TPU v7x, 512 devices: a whole 4x4x16 slice. The times are simulated.
512 devices in a mesh: gx: 16 (over z), gy: 4 (over x), gz: 8 (over y, core).
Axes of the slice: x: 4, y: 4, z: 16, core: 2. Of those that a mesh axis runs over, the one named last changes fastest.
Arguments:
- flow: float32 [4, 128, 64, 1024], P(None, 'gx', 'gy', 'gz'), may hold values from -3 to 3
- basis: float32 [127, 3, 131072], P(None, None, ('gx', 'gy', 'gz')), may hold values from -1150 to 1150
- sample: int32 [131072], P(('gx', 'gy', 'gz')), may hold values from 0 to 16383
Outputs:
- flow_next: float32 [4, 128, 64, 1024], P(None, 'gx', 'gy', 'gz')
- basis_next: float32 [128, 3, 131072], P(None, None, ('gx', 'gy', 'gz'))
- factor: float32 [128, 128], replicated
All inputs are finite; a program needn't handle non-finite values.
Results may differ from a plain program's by a relative error of at most 0.000065.
Values sent between devices are 32-bit elements; how exact they have to be, the bound alone decides.
A program may use at most 64 MiB of HBM per device.

v0:
```python
import jax
import jax.numpy as jnp
from jax import lax
from jax.sharding import PartitionSpec as P

DT_STEP = 0.35
VISCOSITY = 0.2
SOUND_SQ = 1.0
DRIVING = 0.5


def padded(block, sides, width, periodic):
    for axis, dim in sides:
        count = lax.axis_size(axis)
        forward = [(i, i + 1) for i in range(count - 1)]
        if periodic:
            forward.append((count - 1, 0))
        backward = [(target, source) for source, target in forward]
        low = lax.ppermute(
            lax.slice_in_dim(block, block.shape[dim] - width, None, axis=dim), axis, forward
        )
        high = lax.ppermute(lax.slice_in_dim(block, 0, width, axis=dim), axis, backward)
        block = jnp.concatenate([low, block, high], axis=dim)
    return block


def rates(ext):
    centre = ext[:, 1:-1, 1:-1, 1:-1]
    x_plus = ext[:, 2:, 1:-1, 1:-1]
    x_minus = ext[:, :-2, 1:-1, 1:-1]
    y_plus = ext[:, 1:-1, 2:, 1:-1]
    y_minus = ext[:, 1:-1, :-2, 1:-1]
    z_plus = ext[:, 1:-1, 1:-1, 2:]
    z_minus = ext[:, 1:-1, 1:-1, :-2]
    slope_x = 0.5 * (x_plus - x_minus)
    slope_y = 0.5 * (y_plus - y_minus)
    slope_z = 0.5 * (z_plus - z_minus)
    laplace = x_plus + x_minus + (y_plus + y_minus) + (z_plus + z_minus) - 6.0 * centre
    advect = centre[0] * slope_x[:3] + centre[1] * slope_y[:3] + centre[2] * slope_z[:3]
    pressure = jnp.stack([slope_x[3], slope_y[3], slope_z[3]])
    forcing = jnp.array([DRIVING, 0.0, 0.0], dtype=jnp.float32).reshape(3, 1, 1, 1)
    velocity = VISCOSITY * laplace[:3] - advect - pressure + forcing
    density = -SOUND_SQ * (slope_x[0] + slope_y[1] + slope_z[2])
    return jnp.concatenate([velocity, density[None]], axis=0)


def extend_one(fields):
    walled = padded(fields, (("gy", 2),), 1, False)
    return padded(walled, (("gx", 1), ("gz", 3)), 1, True)


def local(flow, basis, sample):
    points = basis.shape[2]
    modes = basis.shape[0]
    count = 3.0 * points * lax.axis_size("gx") * lax.axis_size("gy") * lax.axis_size("gz")
    section_one = flow + DT_STEP * rates(extend_one(flow))
    section_two = 0.75 * flow + 0.25 * (section_one + DT_STEP * rates(extend_one(section_one)))
    flow_next = 1.0 / 3.0 * flow + 2.0 / 3.0 * (
        section_two + DT_STEP * rates(extend_one(section_two))
    )
    velocity = flow_next[:3].reshape(3, -1)
    snapshot = jnp.take(velocity, sample, axis=1)
    stacked = jnp.concatenate([basis, snapshot[None]], axis=0).reshape(modes + 1, 3 * points)
    local_gram = jnp.dot(
        stacked, stacked.T, precision=lax.Precision.HIGHEST, preferred_element_type=jnp.float32
    )
    gram = lax.psum(local_gram, ("gx", "gy", "gz")) / count
    lower = jnp.linalg.cholesky(gram)
    basis_next = jax.scipy.linalg.solve_triangular(lower, stacked, lower=True).reshape(
        modes + 1, 3, points
    )
    return (flow_next, basis_next, lower.T)


def solution(mesh):
    return jax.shard_map(
        local,
        mesh=mesh,
        in_specs=(
            P(None, "gx", "gy", "gz"),
            P(None, None, ("gx", "gy", "gz")),
            P(("gx", "gy", "gz")),
        ),
        out_specs=(P(None, "gx", "gy", "gz"), P(None, None, ("gx", "gy", "gz")), P()),
        check_vma=False,
    )
```

profile of v0, /device:TPU:1, one launch (start us, length us, event | category | flops | bytes accessed | tf_op | source)
XLA Modules:
  0.0 582.4 jit_solution(7620865436270588193)
XLA Ops:
  7.2 1.0 fusion.68
  8.3 3.9 collective-permute-start
  12.2 1.3 collective-permute-start.1
  13.5 0.9 slice_bitcast_fusion.8
  14.4 2.2 collective-permute-done.1
  16.7 0.8 pad_maximum_fusion.64
  17.5 11.1 %collective-permute-start.2 = (f32[4,1,18,128]{3,2,1,0:T(8,128)S(1)}, f32[4,1,18,128]{3,2,1,0:T(8,128)S(1)}, u32[]{:S(2)}, u32[]{:S(2)}) collective-permute-start(f32[4,1,18,128]{3,2,1,0:T(8,128)S(1)} %get-tuple-element.41), channel_id=1, source_target_pairs={{32,0},{64,32},{96,64},{128,96},{160,128},{192,160},{224,192},{256... | collective-permute-start | bytes 110600 | tf_op jit(solution)/shard_map/ppermute | solution.py:22
  28.6 1.9 collective-permute-start.3
  30.6 0.7 compare_select_fusion
  31.2 3.4 collective-permute-done.3
  34.7 1.0 pad_maximum_fusion
  35.9 3.5 collective-permute-start.4
  39.4 1.2 collective-permute-start.5
  40.6 1.6 subtract_multiply_fusion.5
  42.2 5.2 collective-permute-done.4
  47.4 1.4 subtract_multiply_fusion.4
  48.9 1.5 fusion.24
  50.4 3.1 collective-permute-start.6
  53.6 1.3 collective-permute-start.7
  54.9 3.1 collective-permute-done.7
  58.1 1.9 collective-permute-start.8
  60.0 3.4 collective-permute-start.9
  63.4 2.6 collective-permute-done.9
  66.3 4.2 collective-permute-start.10
  70.7 6.5 %collective-permute-done.10 = f32[4,10,18,1]{3,2,1,0:T(8,128)S(1)} collective-permute-done((f32[4,10,18,1]{3,2,1,0:T(8,128)S(1)}, f32[4,10,18,1]{3,2,1,0:T(8,128)S(1)}, u32[]{:S(2)}, u32[]{:S(2)}) %collective-permute-start.10) | collective-permute-done | bytes 2912 | tf_op jit(solution)/shard_map/ppermute | solution.py:22
  77.2 0.3 subtract_multiply_fusion.2
  77.9 2.8 collective-permute-start.12
  80.7 1.3 collective-permute-start.13
  82.2 3.0 collective-permute-done.13
  85.2 1.9 collective-permute-start.14
  87.1 3.5 collective-permute-start.15
  90.7 2.5 collective-permute-done.15
  93.4 5.4 collective-permute-start.16
  99.0 5.4 collective-permute-done.16
  104.5 0.2 collective-permute-done.17
  104.7 0.3 subtract_multiply_fusion
  105.3 4.7 copy.16
  110.1 4.1 gather_fusion
  114.3 1.1 convolution_bitcast_fusion
  115.8 433.0 %all-reduce.2.cloned.1.call-done = f32[128,128]{0,1:T(8,128)} async-done(((f32[128,128]{0,1:T(8,128)}), f32[128,128]{0,1:T(8,128)}) %all-reduce.2.cloned.1.call-update) | async-done | bytes 65552 | tf_op jit(solution)/shard_map/psum | solution.py:67
  548.8 0.8 broadcast_multiply_fusion
  549.8 0.9 fusion.57
  550.6 11.7 %cholesky.16 = f32[128,128]{1,0:T(8,128)S(1)} custom-call(f32[128,128]{1,0:T(8,128)S(1)} %fusion.57), custom_call_target="Cholesky" | custom-call | tf_op jit(solution)/shard_map/jit(cholesky)/cholesky | solution.py:68
  562.4 0.6 compare_reduce_fusion
  563.0 0.7 fusion.58
  563.7 9.8 %custom-call.7 = f32[1,128,128]{1,2,0:T(8,128)S(1)} custom-call(f32[1,128,128]{2,1,0:T(8,128)S(1)} %get-tuple-element.70), custom_call_target="InvertDiagBlocksLowerTriangular" | custom-call | tf_op jit(solution)/shard_map/jit(_solve_triangular)/triangular_solve | solution.py:69
  573.5 0.7 copy.23
  574.2 1.3 fusion.55
  (55 shorter events, 2.6 us)
Async XLA Ops:
  7.2 43.2 %copy-start = (f32[4,8,16,128]{3,2,1,0:T(8,128)S(1)}, f32[4,8,16,128]{3,2,1,0:T(8,128)}, u32[]{:S(2)}) copy-start(f32[4,8,16,128]{3,2,1,0:T(8,128)} %param.6) | copy-start | bytes 786436
  7.2 47.7 %copy-start.4 = (s32[256]{0:T(256)S(1)}, s32[256]{0:T(256)}, u32[]{:S(2)}) copy-start(s32[256]{0:T(256)} %param.8) | copy-start | bytes 3076
  7.2 541.6 %all-reduce.2.cloned.1.call-start = ((), (), s32[]{:S(2)}) async-start(), calls=%async_computation | async-start | bytes 131072 | tf_op jit(solution)/shard_map/psum | solution.py:67
  8.3 6.2 %collective-permute-start = (f32[4,8,1,128]{3,2,1,0:T(1,128)S(1)}, f32[4,8,1,128]{3,2,1,0:T(1,128)S(1)}, u32[]{:S(2)}, u32[]{:S(2)}) collective-permute-start(f32[4,8,1,128]{3,2,1,0:T(1,128)S(1)} %get-tuple-element.67), channel_id=1, source_target_pairs={{0,8},{8,16},{16,24},{1,9},{9,17},{17,25},{2,10},{10,18},{18,26},{... | collective-permute-start | bytes 49160 | tf_op jit(solution)/shard_map/ppermute | solution.py:19
  12.2 4.5 collective-permute-start.1
  17.5 13.7 %collective-permute-start.2 = (f32[4,1,18,128]{3,2,1,0:T(8,128)S(1)}, f32[4,1,18,128]{3,2,1,0:T(8,128)S(1)}, u32[]{:S(2)}, u32[]{:S(2)}) collective-permute-start(f32[4,1,18,128]{3,2,1,0:T(8,128)S(1)} %get-tuple-element.41), channel_id=1, source_target_pairs={{32,0},{64,32},{96,64},{128,96},{160,128},{192,160},{224,192},{256... | collective-permute-start | bytes 110600 | tf_op jit(solution)/shard_map/ppermute | solution.py:22
  28.6 6.0 %collective-permute-start.3 = (f32[4,1,18,128]{3,2,1,0:T(8,128)S(1)}, f32[4,1,18,128]{3,2,1,0:T(8,128)S(1)}, u32[]{:S(2)}, u32[]{:S(2)}) collective-permute-start(f32[4,1,18,128]{3,2,1,0:T(8,128)S(1)} %get-tuple-element.40), channel_id=1, source_target_pairs={{0,32},{32,64},{64,96},{96,128},{128,160},{160,192},{192,224},{224... | collective-permute-start | bytes 110600 | tf_op jit(solution)/shard_map/ppermute | solution.py:19
  35.7 41.9 %copy-start.3 = (f32[3]{0:T(128)S(1)}, f32[3]{0:T(128)}, u32[]{:S(2)}) copy-start(f32[3]{0:T(128)} %constant.80.clone) | copy-start | bytes 40
  35.9 11.5 %collective-permute-start.4 = (f32[4,10,18,1]{3,2,1,0:T(8,128)S(1)}, f32[4,10,18,1]{3,2,1,0:T(8,128)S(1)}, u32[]{:S(2)}, u32[]{:S(2)}) collective-permute-start(f32[4,10,18,1]{3,2,1,0:T(8,128)S(1)} %get-tuple-element.31), channel_id=1, source_target_pairs={{1,0},{2,1},{3,2},{4,3},{5,4},{6,5},{7,6},{0,7},{9,8},{10,9},{11,1... | collective-permute-start | bytes 8648 | tf_op jit(solution)/shard_map/ppermute | solution.py:22
  39.4 8.0 %collective-permute-start.5 = (f32[4,10,18,1]{3,2,1,0:T(8,128)S(1)}, f32[4,10,18,1]{3,2,1,0:T(8,128)S(1)}, u32[]{:S(2)}, u32[]{:S(2)}) collective-permute-start(f32[4,10,18,1]{3,2,1,0:T(8,128)S(1)} %get-tuple-element.32), channel_id=1, source_target_pairs={{0,1},{1,2},{2,3},{3,4},{4,5},{5,6},{6,7},{7,0},{8,9},{9,10},{10,1... | collective-permute-start | bytes 8648 | tf_op jit(solution)/shard_map/ppermute | solution.py:19
  42.2 39.8 %copy-start.1 = (f32[127,3,256]{2,0,1:T(8,128)S(1)}, f32[127,3,256]{2,0,1:T(8,128)}, u32[]{:S(2)}) copy-start(f32[127,3,256]{2,0,1:T(8,128)} %param.7) | copy-start | bytes 1170436
  50.4 4.5 collective-permute-start.6
  53.6 4.5 collective-permute-start.7
  58.1 5.3 collective-permute-start.8
  60.0 6.0 %collective-permute-start.9 = (f32[4,1,18,128]{3,2,1,0:T(8,128)S(1)}, f32[4,1,18,128]{3,2,1,0:T(8,128)S(1)}, u32[]{:S(2)}, u32[]{:S(2)}) collective-permute-start(f32[4,1,18,128]{3,2,1,0:T(8,128)S(1)} %get-tuple-element.37), channel_id=1, source_target_pairs={{0,32},{32,64},{64,96},{96,128},{128,160},{160,192},{192,224},{224... | collective-permute-start | bytes 110600 | tf_op jit(solution)/shard_map/ppermute | solution.py:19
  66.3 10.9 %collective-permute-start.10 = (f32[4,10,18,1]{3,2,1,0:T(8,128)S(1)}, f32[4,10,18,1]{3,2,1,0:T(8,128)S(1)}, u32[]{:S(2)}, u32[]{:S(2)}) collective-permute-start(f32[4,10,18,1]{3,2,1,0:T(8,128)S(1)} %get-tuple-element.29), channel_id=1, source_target_pairs={{1,0},{2,1},{3,2},{4,3},{5,4},{6,5},{7,6},{0,7},{9,8},{10,9},{11,1... | collective-permute-start | bytes 8648 | tf_op jit(solution)/shard_map/ppermute | solution.py:22
  70.5 6.6 %collective-permute-start.11 = (f32[4,10,18,1]{3,2,1,0:T(8,128)S(1)}, f32[4,10,18,1]{3,2,1,0:T(8,128)S(1)}, u32[]{:S(2)}, u32[]{:S(2)}) collective-permute-start(f32[4,10,18,1]{3,2,1,0:T(8,128)S(1)} %get-tuple-element.30), channel_id=1, source_target_pairs={{0,1},{1,2},{2,3},{3,4},{4,5},{5,6},{6,7},{7,0},{8,9},{9,10},{10,1... | collective-permute-start | bytes 8648 | tf_op jit(solution)/shard_map/ppermute | solution.py:19
  77.9 4.3 collective-permute-start.12
  80.7 4.5 collective-permute-start.13
  85.2 5.5 collective-permute-start.14
  87.1 6.0 %collective-permute-start.15 = (f32[4,1,18,128]{3,2,1,0:T(8,128)S(1)}, f32[4,1,18,128]{3,2,1,0:T(8,128)S(1)}, u32[]{:S(2)}, u32[]{:S(2)}) collective-permute-start(f32[4,1,18,128]{3,2,1,0:T(8,128)S(1)} %get-tuple-element.34), channel_id=1, source_target_pairs={{0,32},{32,64},{64,96},{96,128},{128,160},{160,192},{192,224},{224... | collective-permute-start | bytes 110600 | tf_op jit(solution)/shard_map/ppermute | solution.py:19
  93.4 11.0 %collective-permute-start.16 = (f32[4,10,18,1]{3,2,1,0:T(8,128)S(1)}, f32[4,10,18,1]{3,2,1,0:T(8,128)S(1)}, u32[]{:S(2)}, u32[]{:S(2)}) collective-permute-start(f32[4,10,18,1]{3,2,1,0:T(8,128)S(1)} %get-tuple-element.27), channel_id=1, source_target_pairs={{1,0},{2,1},{3,2},{4,3},{5,4},{6,5},{7,6},{0,7},{9,8},{10,9},{11,1... | collective-permute-start | bytes 8648 | tf_op jit(solution)/shard_map/ppermute | solution.py:22
  98.9 5.8 collective-permute-start.17
  105.3 470.2 %copy-start.2 = (f32[4,8,16,128]{3,2,1,0:T(8,128)}, f32[4,8,16,128]{3,2,1,0:T(8,128)S(1)}, u32[]{:S(2)}) copy-start(f32[4,8,16,128]{3,2,1,0:T(8,128)S(1)} %fusion.15) | copy-start | bytes 786436
Sparse Core Ops, SparseCore 0:
  115.5 433.2 all-reduce.1
where the time goes:
time: 583 us; the launch traced here: 582 us
  waiting for transfers between devices  467 us (80%)
  starting transfers between devices  52 us (9%)
  other arithmetic  33.4 us (6%)
  between operations  14.5 us (2%)
  local copies, waits for them, and re-layouts  12.7 us (2%)
    psum x1, waiting for transfers between devices, local(): gram = lax.psum(local_gram, ('gx', 'gy', 'gz')) / count  433 us
    ppermute x9, starting transfers between devices, padded(): lax.ppermute(lax.slice_in_dim(block, 0, width, axis=dim), axis, backward)  32.1 us
    ppermute x9, waiting for transfers between devices, padded(): lax.ppermute(lax.slice_in_dim(block, 0, width, axis=dim), axis, backward)  25.5 us
    ppermute x9, starting transfers between devices, padded(): lax.ppermute(lax.slice_in_dim(block, block.shape[dim] - width, None, axis...  19.9 us
    another operation x3, other arithmetic, local(): lower = jnp.linalg.cholesky(gram)  12.4 us
  transfers between devices with their start and end apart: 19, of which 11 were waited for; matrix products, arithmetic and copies ran while one was open for 1% of the time, Pallas kernels for 0%

commit v1 on v0

--- a/solution.py
+++ b/solution.py
@@ -64,7 +64,7 @@
     local_gram = jnp.dot(
         stacked, stacked.T, precision=lax.Precision.HIGHEST, preferred_element_type=jnp.float32
     )
-    gram = lax.psum(local_gram, ("gx", "gy", "gz")) / count
+    gram = lax.psum(lax.psum(local_gram, "gx"), ("gy", "gz")) / count
     lower = jnp.linalg.cholesky(gram)
     basis_next = jax.scipy.linalg.solve_triangular(lower, stacked, lower=True).reshape(
         modes + 1, 3, points

time: 583 us -> 402 us (0.69)
  waiting for transfers between devices: 467 us -> 286 us
    psum x1 -> x2, waiting for transfers between devices: 433 us -> 252 us  [local(): gram = lax.psum(lax.psum(local_gram, 'gx'), ('gy', 'gz')) / count]
  transfers between devices with their start and end apart: 19 -> 20, of which waited for: 11 -> 12; matrix products, arithmetic and copies ran while one was open for 1% -> 1% of each run, Pallas kernels for 0% -> 0%
where the time goes in v1:
time: 402 us; the launch traced here: 401 us
  waiting for transfers between devices  286 us (71%)
  starting transfers between devices  52.1 us (13%)
  other arithmetic  33.4 us (8%)
  between operations  14.5 us (4%)
  local copies, waits for them, and re-layouts  12.7 us (3%)
    psum x2, waiting for transfers between devices, local(): gram = lax.psum(lax.psum(local_gram, 'gx'), ('gy', 'gz')) / count  252 us
    ppermute x9, starting transfers between devices, padded(): lax.ppermute(lax.slice_in_dim(block, 0, width, axis=dim), axis, backward)  32.1 us
    ppermute x9, waiting for transfers between devices, padded(): lax.ppermute(lax.slice_in_dim(block, 0, width, axis=dim), axis, backward)  25.5 us
    ppermute x9, starting transfers between devices, padded(): lax.ppermute(lax.slice_in_dim(block, block.shape[dim] - width, None, axis...  19.7 us
    another operation x3, other arithmetic, local(): lower = jnp.linalg.cholesky(gram)  12.4 us
    another operation x1, other arithmetic, local(): jax.scipy.linalg.solve_triangular(lower, stacked, lower=True)  9.81 us
    ppermute x9, waiting for transfers between devices, padded(): lax.ppermute(lax.slice_in_dim(block, block.shape[dim] - width, None, axis...  8.92 us
  transfers between devices with their start and end apart: 20, of which 12 were waited for; matrix products, arithmetic and copies ran while one was open for 1% of the time, Pallas kernels for 0%

profile of v1, /device:TPU:1, one launch (start us, length us, event | category | flops | bytes accessed | tf_op | source)
XLA Modules:
  0.0 401.5 jit_solution(337048168244483214)
XLA Ops:
  7.2 1.0 fusion.68
  8.3 3.9 collective-permute-start
  12.2 1.3 collective-permute-start.1
  13.5 0.9 slice_bitcast_fusion.8
  14.4 2.2 collective-permute-done.1
  16.7 0.8 pad_maximum_fusion.64
  17.5 11.1 %collective-permute-start.2 = (f32[4,1,18,128]{3,2,1,0:T(8,128)S(1)}, f32[4,1,18,128]{3,2,1,0:T(8,128)S(1)}, u32[]{:S(2)}, u32[]{:S(2)}) collective-permute-start(f32[4,1,18,128]{3,2,1,0:T(8,128)S(1)} %get-tuple-element.41), channel_id=1, source_target_pairs={{32,0},{64,32},{96,64},{128,96},{160,128},{192,160},{224,192},{256... | collective-permute-start | bytes 110600 | tf_op jit(solution)/shard_map/ppermute | solution.py:22
  28.6 1.9 collective-permute-start.3
  30.6 0.7 compare_select_fusion
  31.2 3.4 collective-permute-done.3
  34.7 1.0 pad_maximum_fusion
  35.9 3.5 collective-permute-start.4
  39.4 1.2 collective-permute-start.5
  40.6 1.6 subtract_multiply_fusion.5
  42.2 5.2 %collective-permute-done.4 = f32[4,10,18,1]{3,2,1,0:T(8,128)S(1)} collective-permute-done((f32[4,10,18,1]{3,2,1,0:T(8,128)S(1)}, f32[4,10,18,1]{3,2,1,0:T(8,128)S(1)}, u32[]{:S(2)}, u32[]{:S(2)}) %collective-permute-start.4) | collective-permute-done | bytes 2912 | tf_op jit(solution)/shard_map/ppermute | solution.py:22
  47.4 1.4 subtract_multiply_fusion.4
  48.9 1.5 fusion.24
  50.4 3.1 collective-permute-start.6
  53.6 1.3 collective-permute-start.7
  54.9 3.1 collective-permute-done.7
  58.1 1.9 collective-permute-start.8
  60.0 3.4 collective-permute-start.9
  63.4 2.6 collective-permute-done.9
  66.3 4.2 %collective-permute-start.10 = (f32[4,10,18,1]{3,2,1,0:T(8,128)S(1)}, f32[4,10,18,1]{3,2,1,0:T(8,128)S(1)}, u32[]{:S(2)}, u32[]{:S(2)}) collective-permute-start(f32[4,10,18,1]{3,2,1,0:T(8,128)S(1)} %get-tuple-element.29), channel_id=1, source_target_pairs={{1,0},{2,1},{3,2},{4,3},{5,4},{6,5},{7,6},{0,7},{9,8},{10,9},{11,1... | collective-permute-start | bytes 8648 | tf_op jit(solution)/shard_map/ppermute | solution.py:22
  70.7 6.5 %collective-permute-done.10 = f32[4,10,18,1]{3,2,1,0:T(8,128)S(1)} collective-permute-done((f32[4,10,18,1]{3,2,1,0:T(8,128)S(1)}, f32[4,10,18,1]{3,2,1,0:T(8,128)S(1)}, u32[]{:S(2)}, u32[]{:S(2)}) %collective-permute-start.10) | collective-permute-done | bytes 2912 | tf_op jit(solution)/shard_map/ppermute | solution.py:22
  77.2 0.3 subtract_multiply_fusion.2
  77.9 2.8 collective-permute-start.12
  80.7 1.3 collective-permute-start.13
  82.2 3.0 collective-permute-done.13
  85.2 1.9 collective-permute-start.14
  87.1 3.4 collective-permute-start.15
  90.5 2.6 collective-permute-done.15
  93.4 5.4 %collective-permute-start.16 = (f32[4,10,18,1]{3,2,1,0:T(8,128)S(1)}, f32[4,10,18,1]{3,2,1,0:T(8,128)S(1)}, u32[]{:S(2)}, u32[]{:S(2)}) collective-permute-start(f32[4,10,18,1]{3,2,1,0:T(8,128)S(1)} %get-tuple-element.27), channel_id=1, source_target_pairs={{1,0},{2,1},{3,2},{4,3},{5,4},{6,5},{7,6},{0,7},{9,8},{10,9},{11,1... | collective-permute-start | bytes 8648 | tf_op jit(solution)/shard_map/ppermute | solution.py:22
  99.0 5.4 %collective-permute-done.16 = f32[4,10,18,1]{3,2,1,0:T(8,128)S(1)} collective-permute-done((f32[4,10,18,1]{3,2,1,0:T(8,128)S(1)}, f32[4,10,18,1]{3,2,1,0:T(8,128)S(1)}, u32[]{:S(2)}, u32[]{:S(2)}) %collective-permute-start.16) | collective-permute-done | bytes 2912 | tf_op jit(solution)/shard_map/ppermute | solution.py:22
  104.7 0.3 subtract_multiply_fusion
  105.3 4.7 %copy.16 = f32[3,8,16,128]{0,3,2,1:T(8,128)} copy(f32[3,8,16,128]{3,2,1,0:T(8,128)S(1)} %slice.406) | data formatting | bytes 393216 | tf_op jit(solution)/shard_map/slice | solution.py:61
  110.1 4.1 %gather_fusion = f32[256,3]{1,0:T(8,128)S(1)} fusion(f32[3,16384]{0,1:T(8,128)} %bitcast.47, s32[1024]{0:T(1024)S(1)} %pad_clamp_fusion), kind=kCustom, calls=%fused_computation | custom fusion | bytes 7168 | tf_op jit(solution)/shard_map/jit(_take)/gather | solution.py:62
  114.2 1.1 convolution_bitcast_fusion
  115.8 115.1 %all-reduce.3.cloned.1.call-done = f32[128,128]{0,1:T(8,128)} async-done(((f32[128,128]{0,1:T(8,128)}), f32[128,128]{0,1:T(8,128)}) %all-reduce.3.cloned.1.call-update) | async-done | bytes 65552 | tf_op jit(solution)/shard_map/psum | solution.py:67
  231.1 136.8 %all-reduce.5.cloned.1.call-done = f32[128,128]{0,1:T(8,128)} async-done(((f32[128,128]{0,1:T(8,128)}), f32[128,128]{0,1:T(8,128)}) %all-reduce.5.cloned.1.call-update) | async-done | bytes 65552 | tf_op jit(solution)/shard_map/psum | solution.py:67
  368.0 0.8 broadcast_multiply_fusion
  368.9 0.9 fusion.57
  369.8 11.7 %cholesky.16 = f32[128,128]{1,0:T(8,128)S(1)} custom-call(f32[128,128]{1,0:T(8,128)S(1)} %fusion.57), custom_call_target="Cholesky" | custom-call | tf_op jit(solution)/shard_map/jit(cholesky)/cholesky | solution.py:68
  381.5 0.6 compare_reduce_fusion
  382.2 0.7 fusion.58
  382.8 9.8 %custom-call.7 = f32[1,128,128]{1,2,0:T(8,128)S(1)} custom-call(f32[1,128,128]{2,1,0:T(8,128)S(1)} %get-tuple-element.70), custom_call_target="InvertDiagBlocksLowerTriangular" | custom-call | tf_op jit(solution)/shard_map/jit(_solve_triangular)/triangular_solve | solution.py:69
  392.7 0.7 copy.23
  393.4 1.3 fusion.55
  (58 shorter events, 3.0 us)
Async XLA Ops:
  7.2 43.2 %copy-start = (f32[4,8,16,128]{3,2,1,0:T(8,128)S(1)}, f32[4,8,16,128]{3,2,1,0:T(8,128)}, u32[]{:S(2)}) copy-start(f32[4,8,16,128]{3,2,1,0:T(8,128)} %param.6) | copy-start | bytes 786436
  7.2 47.7 %copy-start.4 = (s32[256]{0:T(256)S(1)}, s32[256]{0:T(256)}, u32[]{:S(2)}) copy-start(s32[256]{0:T(256)} %param.8) | copy-start | bytes 3076
  7.2 223.7 %all-reduce.3.cloned.1.call-start = ((), (), s32[]{:S(2)}) async-start(), calls=%async_computation | async-start | bytes 131072 | tf_op jit(solution)/shard_map/psum | solution.py:67
  8.3 6.2 %collective-permute-start = (f32[4,8,1,128]{3,2,1,0:T(1,128)S(1)}, f32[4,8,1,128]{3,2,1,0:T(1,128)S(1)}, u32[]{:S(2)}, u32[]{:S(2)}) collective-permute-start(f32[4,8,1,128]{3,2,1,0:T(1,128)S(1)} %get-tuple-element.67), channel_id=1, source_target_pairs={{0,8},{8,16},{16,24},{1,9},{9,17},{17,25},{2,10},{10,18},{18,26},{... | collective-permute-start | bytes 49160 | tf_op jit(solution)/shard_map/ppermute | solution.py:19
  12.2 4.5 %collective-permute-start.1 = (f32[4,8,1,128]{3,2,1,0:T(1,128)S(1)}, f32[4,8,1,128]{3,2,1,0:T(1,128)S(1)}, u32[]{:S(2)}, u32[]{:S(2)}) collective-permute-start(f32[4,8,1,128]{3,2,1,0:T(1,128)S(1)} %get-tuple-element.68), channel_id=1, source_target_pairs={{8,0},{16,8},{24,16},{9,1},{17,9},{25,17},{10,2},{18,10},{26,18},{... | collective-permute-start | bytes 49160 | tf_op jit(solution)/shard_map/ppermute | solution.py:22
  17.5 13.7 %collective-permute-start.2 = (f32[4,1,18,128]{3,2,1,0:T(8,128)S(1)}, f32[4,1,18,128]{3,2,1,0:T(8,128)S(1)}, u32[]{:S(2)}, u32[]{:S(2)}) collective-permute-start(f32[4,1,18,128]{3,2,1,0:T(8,128)S(1)} %get-tuple-element.41), channel_id=1, source_target_pairs={{32,0},{64,32},{96,64},{128,96},{160,128},{192,160},{224,192},{256... | collective-permute-start | bytes 110600 | tf_op jit(solution)/shard_map/ppermute | solution.py:22
  28.6 6.0 %collective-permute-start.3 = (f32[4,1,18,128]{3,2,1,0:T(8,128)S(1)}, f32[4,1,18,128]{3,2,1,0:T(8,128)S(1)}, u32[]{:S(2)}, u32[]{:S(2)}) collective-permute-start(f32[4,1,18,128]{3,2,1,0:T(8,128)S(1)} %get-tuple-element.40), channel_id=1, source_target_pairs={{0,32},{32,64},{64,96},{96,128},{128,160},{160,192},{192,224},{224... | collective-permute-start | bytes 110600 | tf_op jit(solution)/shard_map/ppermute | solution.py:19
  35.7 41.9 %copy-start.3 = (f32[3]{0:T(128)S(1)}, f32[3]{0:T(128)}, u32[]{:S(2)}) copy-start(f32[3]{0:T(128)} %constant.80.clone) | copy-start | bytes 40
  35.9 11.5 %collective-permute-start.4 = (f32[4,10,18,1]{3,2,1,0:T(8,128)S(1)}, f32[4,10,18,1]{3,2,1,0:T(8,128)S(1)}, u32[]{:S(2)}, u32[]{:S(2)}) collective-permute-start(f32[4,10,18,1]{3,2,1,0:T(8,128)S(1)} %get-tuple-element.31), channel_id=1, source_target_pairs={{1,0},{2,1},{3,2},{4,3},{5,4},{6,5},{7,6},{0,7},{9,8},{10,9},{11,1... | collective-permute-start | bytes 8648 | tf_op jit(solution)/shard_map/ppermute | solution.py:22
  39.4 8.0 %collective-permute-start.5 = (f32[4,10,18,1]{3,2,1,0:T(8,128)S(1)}, f32[4,10,18,1]{3,2,1,0:T(8,128)S(1)}, u32[]{:S(2)}, u32[]{:S(2)}) collective-permute-start(f32[4,10,18,1]{3,2,1,0:T(8,128)S(1)} %get-tuple-element.32), channel_id=1, source_target_pairs={{0,1},{1,2},{2,3},{3,4},{4,5},{5,6},{6,7},{7,0},{8,9},{9,10},{10,1... | collective-permute-start | bytes 8648 | tf_op jit(solution)/shard_map/ppermute | solution.py:19
  42.2 39.8 %copy-start.1 = (f32[127,3,256]{2,0,1:T(8,128)S(1)}, f32[127,3,256]{2,0,1:T(8,128)}, u32[]{:S(2)}) copy-start(f32[127,3,256]{2,0,1:T(8,128)} %param.7) | copy-start | bytes 1170436
  50.4 4.5 %collective-permute-start.6 = (f32[4,8,1,128]{3,2,1,0:T(1,128)S(1)}, f32[4,8,1,128]{3,2,1,0:T(1,128)S(1)}, u32[]{:S(2)}, u32[]{:S(2)}) collective-permute-start(f32[4,8,1,128]{3,2,1,0:T(1,128)S(1)} %get-tuple-element.58), channel_id=1, source_target_pairs={{0,8},{8,16},{16,24},{1,9},{9,17},{17,25},{2,10},{10,18},{18,26},{... | collective-permute-start | bytes 49160 | tf_op jit(solution)/shard_map/ppermute | solution.py:19
  53.6 4.5 %collective-permute-start.7 = (f32[4,8,1,128]{3,2,1,0:T(1,128)S(1)}, f32[4,8,1,128]{3,2,1,0:T(1,128)S(1)}, u32[]{:S(2)}, u32[]{:S(2)}) collective-permute-start(f32[4,8,1,128]{3,2,1,0:T(1,128)S(1)} %get-tuple-element.59), channel_id=1, source_target_pairs={{8,0},{16,8},{24,16},{9,1},{17,9},{25,17},{10,2},{18,10},{26,18},{... | collective-permute-start | bytes 49160 | tf_op jit(solution)/shard_map/ppermute | solution.py:22
  58.1 5.3 %collective-permute-start.8 = (f32[4,1,18,128]{3,2,1,0:T(8,128)S(1)}, f32[4,1,18,128]{3,2,1,0:T(8,128)S(1)}, u32[]{:S(2)}, u32[]{:S(2)}) collective-permute-start(f32[4,1,18,128]{3,2,1,0:T(8,128)S(1)} %get-tuple-element.38), channel_id=1, source_target_pairs={{32,0},{64,32},{96,64},{128,96},{160,128},{192,160},{224,192},{256... | collective-permute-start | bytes 110600 | tf_op jit(solution)/shard_map/ppermute | solution.py:22
  60.0 6.0 %collective-permute-start.9 = (f32[4,1,18,128]{3,2,1,0:T(8,128)S(1)}, f32[4,1,18,128]{3,2,1,0:T(8,128)S(1)}, u32[]{:S(2)}, u32[]{:S(2)}) collective-permute-start(f32[4,1,18,128]{3,2,1,0:T(8,128)S(1)} %get-tuple-element.37), channel_id=1, source_target_pairs={{0,32},{32,64},{64,96},{96,128},{128,160},{160,192},{192,224},{224... | collective-permute-start | bytes 110600 | tf_op jit(solution)/shard_map/ppermute | solution.py:19
  66.3 10.9 %collective-permute-start.10 = (f32[4,10,18,1]{3,2,1,0:T(8,128)S(1)}, f32[4,10,18,1]{3,2,1,0:T(8,128)S(1)}, u32[]{:S(2)}, u32[]{:S(2)}) collective-permute-start(f32[4,10,18,1]{3,2,1,0:T(8,128)S(1)} %get-tuple-element.29), channel_id=1, source_target_pairs={{1,0},{2,1},{3,2},{4,3},{5,4},{6,5},{7,6},{0,7},{9,8},{10,9},{11,1... | collective-permute-start | bytes 8648 | tf_op jit(solution)/shard_map/ppermute | solution.py:22
  70.5 6.6 %collective-permute-start.11 = (f32[4,10,18,1]{3,2,1,0:T(8,128)S(1)}, f32[4,10,18,1]{3,2,1,0:T(8,128)S(1)}, u32[]{:S(2)}, u32[]{:S(2)}) collective-permute-start(f32[4,10,18,1]{3,2,1,0:T(8,128)S(1)} %get-tuple-element.30), channel_id=1, source_target_pairs={{0,1},{1,2},{2,3},{3,4},{4,5},{5,6},{6,7},{7,0},{8,9},{9,10},{10,1... | collective-permute-start | bytes 8648 | tf_op jit(solution)/shard_map/ppermute | solution.py:19
  77.9 4.3 %collective-permute-start.12 = (f32[4,8,1,128]{3,2,1,0:T(1,128)S(1)}, f32[4,8,1,128]{3,2,1,0:T(1,128)S(1)}, u32[]{:S(2)}, u32[]{:S(2)}) collective-permute-start(f32[4,8,1,128]{3,2,1,0:T(1,128)S(1)} %get-tuple-element.49), channel_id=1, source_target_pairs={{0,8},{8,16},{16,24},{1,9},{9,17},{17,25},{2,10},{10,18},{18,26},{... | collective-permute-start | bytes 49160 | tf_op jit(solution)/shard_map/ppermute | solution.py:19
  80.7 4.5 %collective-permute-start.13 = (f32[4,8,1,128]{3,2,1,0:T(1,128)S(1)}, f32[4,8,1,128]{3,2,1,0:T(1,128)S(1)}, u32[]{:S(2)}, u32[]{:S(2)}) collective-permute-start(f32[4,8,1,128]{3,2,1,0:T(1,128)S(1)} %get-tuple-element.50), channel_id=1, source_target_pairs={{8,0},{16,8},{24,16},{9,1},{17,9},{25,17},{10,2},{18,10},{26,18},{... | collective-permute-start | bytes 49160 | tf_op jit(solution)/shard_map/ppermute | solution.py:22
  85.2 5.3 %collective-permute-start.14 = (f32[4,1,18,128]{3,2,1,0:T(8,128)S(1)}, f32[4,1,18,128]{3,2,1,0:T(8,128)S(1)}, u32[]{:S(2)}, u32[]{:S(2)}) collective-permute-start(f32[4,1,18,128]{3,2,1,0:T(8,128)S(1)} %get-tuple-element.35), channel_id=1, source_target_pairs={{32,0},{64,32},{96,64},{128,96},{160,128},{192,160},{224,192},{256... | collective-permute-start | bytes 110600 | tf_op jit(solution)/shard_map/ppermute | solution.py:22
  87.1 6.0 %collective-permute-start.15 = (f32[4,1,18,128]{3,2,1,0:T(8,128)S(1)}, f32[4,1,18,128]{3,2,1,0:T(8,128)S(1)}, u32[]{:S(2)}, u32[]{:S(2)}) collective-permute-start(f32[4,1,18,128]{3,2,1,0:T(8,128)S(1)} %get-tuple-element.34), channel_id=1, source_target_pairs={{0,32},{32,64},{64,96},{96,128},{128,160},{160,192},{192,224},{224... | collective-permute-start | bytes 110600 | tf_op jit(solution)/shard_map/ppermute | solution.py:19
  93.4 11.0 %collective-permute-start.16 = (f32[4,10,18,1]{3,2,1,0:T(8,128)S(1)}, f32[4,10,18,1]{3,2,1,0:T(8,128)S(1)}, u32[]{:S(2)}, u32[]{:S(2)}) collective-permute-start(f32[4,10,18,1]{3,2,1,0:T(8,128)S(1)} %get-tuple-element.27), channel_id=1, source_target_pairs={{1,0},{2,1},{3,2},{4,3},{5,4},{6,5},{7,6},{0,7},{9,8},{10,9},{11,1... | collective-permute-start | bytes 8648 | tf_op jit(solution)/shard_map/ppermute | solution.py:22
  98.9 5.8 %collective-permute-start.17 = (f32[4,10,18,1]{3,2,1,0:T(8,128)S(1)}, f32[4,10,18,1]{3,2,1,0:T(8,128)S(1)}, u32[]{:S(2)}, u32[]{:S(2)}) collective-permute-start(f32[4,10,18,1]{3,2,1,0:T(8,128)S(1)} %get-tuple-element.28), channel_id=1, source_target_pairs={{0,1},{1,2},{2,3},{3,4},{4,5},{5,6},{6,7},{7,0},{8,9},{9,10},{10,1... | collective-permute-start | bytes 8648 | tf_op jit(solution)/shard_map/ppermute | solution.py:19
  105.3 289.4 %copy-start.2 = (f32[4,8,16,128]{3,2,1,0:T(8,128)}, f32[4,8,16,128]{3,2,1,0:T(8,128)S(1)}, u32[]{:S(2)}) copy-start(f32[4,8,16,128]{3,2,1,0:T(8,128)S(1)} %fusion.15) | copy-start | bytes 786436
  115.4 252.6 %all-reduce.5.cloned.1.call-start = ((), (), s32[]{:S(2)}) async-start(), calls=%async_computation.1 | async-start | bytes 131072 | tf_op jit(solution)/shard_map/psum | solution.py:67
Sparse Core Ops, SparseCore 0:
  115.5 115.3 all-reduce.2
  234.5 133.4 all-reduce.4
